TPU v7x, 512 devices: a whole 4x4x16 slice. The times are simulated.
512 devices in a mesh: dp: 8 (over y, core), row: 64 (over x, z).
Axes of the slice: x: 4, y: 4, z: 16, core: 2. Of those that a mesh axis runs over, the one named last changes fastest.
Arguments:
- hidden: bfloat16 [8, 128, 128, 768], P('dp', 'row'), may hold values from -6 to 6
- masked: int32 [8, 128, 128], P('dp', 'row'), may hold values 0 or 1
- depths: int32 [8], P('dp'), may hold values from 32 to 128, as said below
- norm_gain: float32 [768], replicated, may hold values from 0.25 to 1.75
- w_query: bfloat16 [768, 768], P('row'), may hold values from -0.21875 to 0.21875
- w_key: bfloat16 [768, 768], P('row'), may hold values from -0.21875 to 0.21875
- w_value: bfloat16 [768, 768], P('row'), may hold values from -0.21875 to 0.21875
- w_out: bfloat16 [768, 768], P('row'), may hold values from -0.21875 to 0.21875
- cotangent: bfloat16 [8, 128, 128, 768], P('dp', 'row'), may hold values from -6 to 6
Outputs:
- mixed: bfloat16 [8, 128, 128, 768], P('dp', 'row')
- grad_hidden: bfloat16 [8, 128, 128, 768], P('dp', 'row')
Inputs may be any that keep to these rules, and one draw needn't show every extreme that they name: `depths`: rows at or past an MSA's depth are padding.
All inputs are finite; a program needn't handle non-finite values. No bound on the sum of `masked` on one device may be relied on, other than what follows from the above.
Results may differ from a plain program's by a relative error of at most 0.0059.
Values may be sent and summed in bfloat16 or wider, within the bound.
A program may use at most 64 MiB of HBM per device.

v0:
```python
import jax
import jax.numpy as jnp
from jax import lax
from jax.sharding import PartitionSpec as P

HEADS = 12


EPS = 1e-05


def softmax_rows(scores):
    top = jnp.max(scores, axis=-1, keepdims=True)
    expo = jnp.exp(scores - top)
    return expo / jnp.sum(expo, axis=-1, keepdims=True)


def back_dot(left, weight):
    return lax.dot_general(
        left, weight, (((1,), (1,)), ((), ())), preferred_element_type=jnp.float32
    )


def body(hidden, masked, depths, norm_gain, w_query, w_key, w_value, w_out, cotangent):
    local_rows = hidden.shape[1]
    columns = hidden.shape[2]
    width = hidden.shape[3]
    head_count = HEADS
    head_size = width // head_count
    flat_rows = local_rows * columns
    first_row = lax.axis_index("row") * local_rows
    depth = depths[0]
    alive = (first_row + jnp.arange(local_rows, dtype=jnp.int32) < depth).astype(jnp.float32)
    mask_rows = masked[0]
    weighting = mask_rows.astype(jnp.float32) * alive[:, None]
    live_total, masked_total = lax.psum(
        (jnp.sum(alive) * columns, jnp.sum(weighting)), ("dp", "row")
    )
    loss_ratio = live_total / jnp.maximum(masked_total, 1.0)
    full_query, full_key, full_value, full_out = (
        lax.all_gather(w_query, "row", axis=0, tiled=True),
        lax.all_gather(w_key, "row", axis=0, tiled=True),
        lax.all_gather(w_value, "row", axis=0, tiled=True),
        lax.all_gather(w_out, "row", axis=0, tiled=True),
    )
    widened = hidden[0].reshape(flat_rows, width).astype(jnp.float32)
    average = jnp.mean(widened, axis=-1, keepdims=True)
    centred = widened - average
    variance = jnp.mean(centred * centred, axis=-1, keepdims=True)
    inv_std = lax.rsqrt(variance + EPS)
    x_hat = centred * inv_std
    normed = (x_hat * norm_gain).astype(jnp.bfloat16)

    def project(weight):
        out = jnp.dot(normed, weight, preferred_element_type=jnp.float32).astype(jnp.bfloat16)
        return out.reshape(local_rows, columns, head_count, head_size)

    queries = project(full_query)
    keys_proj = project(full_key)
    values_proj = project(full_value)
    alive_heads = alive[:, None, None, None]
    query_live = queries * alive_heads.astype(jnp.bfloat16)
    scale = 1.0 / jnp.sqrt(depth.astype(jnp.float32) * head_size)
    partial_value = jnp.einsum(
        "rihe,rjhe->hij", query_live, keys_proj, preferred_element_type=jnp.float32
    )
    logits = lax.psum(partial_value, "row") * scale
    probs = softmax_rows(logits)
    probs_low = probs.astype(jnp.bfloat16)
    attended = jnp.einsum(
        "hij,rjhe->rihe", probs_low, values_proj, preferred_element_type=jnp.float32
    ).astype(jnp.bfloat16)
    projected = jnp.dot(
        attended.reshape(flat_rows, width), full_out, preferred_element_type=jnp.float32
    )
    alive_tokens = jnp.repeat(alive, columns)[:, None]
    mixed = (widened + alive_tokens * projected).astype(jnp.bfloat16)
    back_query, back_key, back_value, back_out = (
        lax.all_gather(w_query, "row", axis=0, tiled=True),
        lax.all_gather(w_key, "row", axis=0, tiled=True),
        lax.all_gather(w_value, "row", axis=0, tiled=True),
        lax.all_gather(w_out, "row", axis=0, tiled=True),
    )
    token_weight = (weighting * loss_ratio).reshape(flat_rows, 1)
    grad_mixed = cotangent[0].reshape(flat_rows, width).astype(jnp.float32) * token_weight
    grad_attended = back_dot(grad_mixed.astype(jnp.bfloat16), back_out).astype(jnp.bfloat16)
    grad_attended = grad_attended.reshape(local_rows, columns, head_count, head_size)
    grad_partial = jnp.einsum(
        "rihe,rjhe->hij", grad_attended, values_proj, preferred_element_type=jnp.float32
    )
    grad_values = jnp.einsum(
        "hij,rihe->rjhe", probs_low, grad_attended, preferred_element_type=jnp.float32
    ).astype(jnp.bfloat16)
    grad_probs = lax.psum(grad_partial, "row")
    grad_logits = probs * (grad_probs - jnp.sum(probs * grad_probs, axis=-1, keepdims=True))
    grad_logits = (grad_logits * scale).astype(jnp.bfloat16)
    grad_queries = (
        jnp.einsum("hij,rjhe->rihe", grad_logits, keys_proj, preferred_element_type=jnp.float32)
        * alive_heads
    ).astype(jnp.bfloat16)
    grad_keys = jnp.einsum(
        "hij,rihe->rjhe", grad_logits, query_live, preferred_element_type=jnp.float32
    ).astype(jnp.bfloat16)
    grad_normed = back_dot(grad_queries.reshape(flat_rows, width), back_query)
    grad_normed = grad_normed + back_dot(grad_keys.reshape(flat_rows, width), back_key)
    grad_normed = grad_normed + back_dot(grad_values.reshape(flat_rows, width), back_value)
    scaled = grad_normed * norm_gain
    grad_x = inv_std * (
        scaled
        - jnp.mean(scaled, axis=-1, keepdims=True)
        - x_hat * jnp.mean(scaled * x_hat, axis=-1, keepdims=True)
    )
    grad_hidden = (grad_mixed + grad_x).astype(jnp.bfloat16)
    return (
        mixed.reshape(1, local_rows, columns, width),
        grad_hidden.reshape(1, local_rows, columns, width),
    )


def solution(mesh):
    return jax.shard_map(
        body,
        mesh=mesh,
        in_specs=(
            P("dp", "row", None, None),
            P("dp", "row", None),
            P("dp"),
            P(),
            P("row", None),
            P("row", None),
            P("row", None),
            P("row", None),
            P("dp", "row", None, None),
        ),
        out_specs=(P("dp", "row", None, None), P("dp", "row", None, None)),
        check_vma=False,
    )
```

profile of v0, /device:TPU:1, one launch (start us, length us, event | category | flops | bytes accessed | tf_op | source)
XLA Modules:
  0.0 904.3 jit_solution(1743458833186725922)
XLA Ops:
  7.2 0.7 all-gather.13.cloned.1.call-update
  8.0 0.7 all-gather.9.cloned.1.call-update
  8.7 0.7 all-gather.11.cloned.1.call-update
  9.4 0.5 all-gather.15.cloned.1.call-update
  10.7 0.6 fusion.67
  11.9 1.9 broadcast_bitcast_fusion
  13.9 111.9 %all-reduce = (f32[]{:T(128)}, f32[]{:T(128)}) all-reduce(f32[]{:T(128)S(6)} %mul.140, f32[]{:T(128)} %get-tuple-element.13), channel_id=1, replica_groups=mesh['dp'=8,'row'=64] {'dp','row'}, use_global_device_ids=true, to_apply=%region_6.0 | all-reduce | flops 2 | bytes 16 | tf_op jit(solution)/shard_map/psum | solution.py:36
  127.0 1.1 convert_reduce_fusion
  128.2 1.2 multiply_reduce_fusion.1
  129.4 0.8 fusion.54
  130.2 0.9 multiply_convert_fusion
  131.1 15.7 %all-gather.13.cloned.1.call-done = bf16[64,12,768]{2,1,0:T(8,128)(2,1)} async-done(((bf16[1,12,768]{2,1,0:T(8,128)(2,1)}), bf16[64,12,768]{2,1,0:T(8,128)(2,1)}) %all-gather.13.cloned.1.call-update) | async-done | bytes 1179664 | tf_op jit(solution)/shard_map/all_gather | solution.py:42
  146.8 2.2 reshape.134
  149.0 0.5 convolution_convert_fusion.1
  149.7 0.8 reshape.119
  150.5 135.5 %all-gather.9.cloned.1.call-done = bf16[64,12,768]{2,1,0:T(8,128)(2,1)} async-done(((bf16[1,12,768]{2,1,0:T(8,128)(2,1)}), bf16[64,12,768]{2,1,0:T(8,128)(2,1)}) %all-gather.9.cloned.1.call-update) | async-done | bytes 1179664 | tf_op jit(solution)/shard_map/all_gather | solution.py:43
  286.0 2.2 reshape.130
  288.3 0.5 convolution_convert_fusion.3
  288.9 0.8 reshape.117
  289.8 135.7 %all-gather.11.cloned.1.call-done = bf16[64,12,768]{2,1,0:T(8,128)(2,1)} async-done(((bf16[1,12,768]{2,1,0:T(8,128)(2,1)}), bf16[64,12,768]{2,1,0:T(8,128)(2,1)}) %all-gather.11.cloned.1.call-update) | async-done | bytes 1179664 | tf_op jit(solution)/shard_map/all_gather | solution.py:41
  425.4 2.2 reshape.132
  427.7 2.2 convolution_convert_fusion.2
  429.9 1.9 copy.35
  431.9 1.8 reshape.118
  433.7 131.0 %all-gather.15.cloned.1.call-done = bf16[64,12,768]{2,1,0:T(8,128)(2,1)} async-done(((bf16[1,12,768]{2,1,0:T(8,128)(2,1)}), bf16[64,12,768]{2,1,0:T(8,128)(2,1)}) %all-gather.15.cloned.1.call-update) | async-done | bytes 1179664 | tf_op jit(solution)/shard_map/all_gather | solution.py:44
  564.7 3.1 reshape.136
  567.9 2.7 convolution_convert_fusion
  570.5 1.9 copy.41
  572.4 1.8 reshape.122
  574.3 1.4 broadcast_multiply_fusion
  575.7 2.5 convolution_bitcast_fusion
  578.2 1.2 convolution_bitcast_fusion.1
  579.5 275.2 %all-reduce.4.cloned.1.call-done = (f32[12,128,128]{2,1,0:T(8,128)}, f32[12,128,128]{2,1,0:T(8,128)}) async-done(((f32[12,128,128]{2,1,0:T(8,128)}, f32[12,128,128]{2,1,0:T(8,128)}), (f32[12,128,128]{2,1,0:T(8,128)}, f32[12,128,128]{2,1,0:T(8,128)})) %all-reduce.4.cloned.1.call-update) | async-done | bytes 1572880 | tf_op jit(solution)/shard_map/psum | solution.py:67
  854.7 2.3 fusion.68
  857.0 10.9 %fusion.15 = bf16[2,128,12,64]{1,3,0,2:T(8,128)(2,1)} fusion(f32[12,128,128]{2,1,0:T(8,128)} %get-tuple-element.7, f32[2]{0:T(128)} %copy-done.10, f32[]{:T(128)S(6)} %sqrt.3, bf16[2,128,12,64]{1,0,3,2:T(2,128)(2,1)} %reshape.119, f32[12,128,128]{2,1,0:T(8,128)} %get-tuple-element.15, f32[12,128]{1,0:T(8,128)S(1)} %get-tuple-element.14), kind=kOutput, calls=%fused_computation.28 | convolution fusion | flops 52102784 | bytes 2365452 | tf_op jit(solution)/shard_map/hij,rjhe->rihe/dot_general | solution.py:98
  867.9 10.9 %fusion.13 = bf16[2,128,12,64]{1,3,0,2:T(8,128)(2,1)} fusion(f32[12,128,128]{2,1,0:T(8,128)} %get-tuple-element.7, f32[]{:T(128)S(6)} %sqrt.3, bf16[2,128,12,64]{1,0,3,2:T(2,128)(2,1)} %copy-done.4, f32[12,128,128]{2,1,0:T(8,128)} %get-tuple-element.15, f32[12,128]{1,0:T(8,128)S(1)} %get-tuple-element.14), kind=kOutput, calls=%fused_computation.26 | convolution fusion | flops 51906176 | bytes 2365444 | tf_op jit(solution)/shard_map/hij,rihe->rjhe/dot_general | solution.py:101
  878.9 4.8 fusion.14
  883.7 4.8 fusion.12
  888.5 1.4 copy.47
  889.9 1.4 copy.45
  891.3 0.5 fusion.32
  891.8 0.5 copy-done.8
  893.2 0.5 convolution_add_fusion.1
  893.7 0.4 copy-done.1
  894.1 0.7 fusion.66
  894.9 0.5 copy-done.5
  895.4 1.3 fusion.9
  896.7 1.1 fusion.19
  (39 shorter events, 1.4 us)
Async XLA Ops:
  7.2 123.0 %copy-start = (bf16[1,2,128,768]{3,2,1,0:T(8,128)(2,1)S(1)}, bf16[1,2,128,768]{3,2,1,0:T(8,128)(2,1)}, u32[]{:S(2)}) copy-start(bf16[1,2,128,768]{3,2,1,0:T(8,128)(2,1)} %param.9) | copy-start | bytes 1179652
  7.2 139.6 %all-gather.13.cloned.1.call-start = ((), (), s32[]{:S(2)}) async-start(), calls=%async_computation.2 | async-start | bytes 1597440 | tf_op jit(solution)/shard_map/all_gather | solution.py:42
  7.9 278.1 %all-gather.9.cloned.1.call-start = ((), (), s32[]{:S(2)}) async-start(), calls=%async_computation | async-start | bytes 1597440 | tf_op jit(solution)/shard_map/all_gather | solution.py:43
  8.7 416.8 %all-gather.11.cloned.1.call-start = ((), (), s32[]{:S(2)}) async-start(), calls=%async_computation.1 | async-start | bytes 1597440 | tf_op jit(solution)/shard_map/all_gather | solution.py:41
  9.4 555.3 %all-gather.15.cloned.1.call-start = ((), (), s32[]{:S(2)}) async-start(), calls=%async_computation.3 | async-start | bytes 1597440 | tf_op jit(solution)/shard_map/all_gather | solution.py:44
  10.0 844.7 %all-reduce.4.cloned.1.call-start = ((), (), s32[]{:S(2)}) async-start(), calls=%async_computation.4 | async-start | bytes 3145728 | tf_op jit(solution)/shard_map/psum | solution.py:67
  11.3 119.8 %copy-start.10 = (f32[2]{0:T(128)}, f32[2]{0:T(128)S(1)}, u32[]{:S(2)}) copy-start(f32[2]{0:T(128)S(1)} %get-tuple-element.9) | copy-start | bytes 28
  130.2 437.7 %copy-start.11 = (f32[256]{0:T(256)}, f32[256]{0:T(256)S(1)}, u32[]{:S(2)}) copy-start(f32[256]{0:T(256)S(1)} %fusion.54) | copy-start | bytes 3076
  131.1 157.2 %copy-start.2 = (bf16[256,768]{1,0:T(8,128)(2,1)}, bf16[256,768]{1,0:T(8,128)(2,1)S(1)}, u32[]{:S(2)}) copy-start(bf16[256,768]{1,0:T(8,128)(2,1)S(1)} %multiply_convert_fusion) | copy-start | bytes 1179652
  574.3 3.9 copy-start.3
  575.7 2.5 copy-start.4
  891.3 1.0 copy-start.8
  891.3 1.4 copy-start.7
  893.1 1.0 copy-start.1
  893.1 1.0 copy-start.9
  894.1 1.3 copy-start.5
  894.1 1.3 copy-start.13
  895.4 1.3 copy-start.6
  895.4 1.3 copy-start.12
Sparse Core Ops, SparseCore 0:
  10.9 135.8 all-gather.12
  149.7 136.2 all-gather.8
  289.0 136.4 all-gather.10
  428.3 136.4 all-gather.14
  579.6 275.1 all-reduce.3
where the time goes:
time: 915 us; the launch traced here: 904 us
  waiting for transfers between devices  696 us (76%)
  blocking collectives  112 us (12%)
  matrix products  44 us (5%)
  local copies, waits for them, and re-layouts  24.6 us (3%)
  between operations  16.6 us (2%)
  other arithmetic  11.4 us (1%)
    psum x1, waiting for transfers between devices, body(): logits = lax.psum(partial_value, 'row') * scale  275 us
    all_gather x1, waiting for transfers between devices, body(): lax.all_gather(w_query, 'row', axis=0, tiled=True)  136 us
    all_gather x1, waiting for transfers between devices, body(): lax.all_gather(w_value, 'row', axis=0, tiled=True)  135 us
    all_gather x1, waiting for transfers between devices, body(): lax.all_gather(w_out, 'row', axis=0, tiled=True)  131 us
    psum x1, blocking collectives, body(): lax.psum((jnp.sum(alive) * columns, jnp.sum(weighting)), ('dp', 'row'))  112 us
  transfers between devices with their start and end apart: 5, of which 5 were waited for; matrix products, arithmetic and copies ran while one was open for 2% of the time, Pallas kernels for 0%

commit v1 on v0

v1 whole, which is shorter than its diff:
```python
import jax
import jax.numpy as jnp
from jax import lax
from jax.experimental import pallas as pl
from jax.experimental.pallas import tpu as pltpu
from jax.sharding import PartitionSpec as P

HEADS = 12
EPS = 1e-05
NX, NY, NZ, NC = 4, 4, 16, 2
D = 768
COLS = 128
SHARD = D // (NX * NZ)
SLAB = SHARD * NZ
HALF = D // NC
HPX = HEADS // NX
IPZ = COLS // NZ
CHUNK = 2 * HPX * IPZ
MESH = pl.DeviceIdType.MESH
BF, F32 = jnp.bfloat16, jnp.float32


def place():
    dp, row = lax.axis_index("dp"), lax.axis_index("row")
    return lax.div(row, NZ), lax.div(dp, NC), lax.rem(row, NZ), lax.rem(dp, NC)


def device(x, y, z, c):
    return (y * NC + c, x * NZ + z)


def mod(a, n):
    return lax.rem(a + n, n)


class Copies:
    def __init__(self, sems):
        self.sems, self.sent = sems, []

    def send(self, src, dst, recv, to):
        copy = pltpu.make_async_remote_copy(
            src_ref=src, dst_ref=dst, send_sem=self.sems.at[len(self.sent)], recv_sem=recv,
            device_id=to, device_id_type=MESH)
        copy.start()
        self.sent.append(copy)

    def drain(self):
        for copy in self.sent:
            copy.wait_send()


def wait_recv(ref, sem):
    pltpu.make_async_copy(ref, ref, sem).wait()


def greet(devices):
    barrier = pltpu.get_barrier_semaphore()
    for to in devices:
        pl.semaphore_signal(barrier, inc=1, device_id=to, device_id_type=MESH)
    pl.semaphore_wait(barrier, len(devices))


def gather_kernel(wq, wk, wv, wo, cnt, full, total, stack, zbuf, cz, cx, cd, cy, tmp, blk,
                  local, zrecv, crecv, frecv, srecv, sibrecv, send_sems):
    x, y, z, c = place()
    loads = [pltpu.make_async_copy(w, stack.at[i], local.at[i]) for i, w in enumerate((wq, wk, wv, wo))]
    for load in loads:
        load.start()
    zs = [device(x, y, mod(z + d, NZ), c) for d in range(1, NZ)]
    xs = [device(mod(x + d, NX), y, z, c) for d in range(1, NX)]
    dps = [device(x, lax.div(e, NC), z, lax.rem(e, NC))
           for e in [mod(y * NC + c + d, NY * NC) for d in range(1, NY * NC)]]
    greet(zs + xs + dps)
    for load in loads:
        load.wait()
    copies = Copies(send_sems)
    mine = stack.at[y, :, pl.ds(pl.multiple_of(c * HALF, HALF), HALF)]
    far = sorted(range(1, NZ), key=lambda d: -min(d, NZ - d))
    for d in far:
        copies.send(mine, zbuf.at[z], zrecv, zs[d - 1])
    for d in far:
        copies.send(cnt, cz.at[z], crecv.at[0], zs[d - 1])
    keep = pltpu.make_async_copy(mine, zbuf.at[z], local.at[0])
    keep.start()
    keepc = pltpu.make_async_copy(cnt, cz.at[z], local.at[1])
    keepc.start()
    keep.wait()
    keepc.wait()
    wait_recv(zbuf.at[pl.ds(0, NZ - 1)], zrecv)
    for i in range(NZ):
        tmp[SHARD * i:SHARD * (i + 1), :] = zbuf[i].astype(F32)
    blk[...] = tmp[...].astype(BF)

    def spot(df, ds, part=None):
        bx = mod(x + df * (1 - c) + ds * c, NX)
        by = mod(y + df * c + ds * (1 - c), NY)
        first, rows = (0, SLAB) if part is None else (part * (SLAB // 2), SLAB // 2)
        return full.at[by, pl.ds(pl.multiple_of(bx * SLAB + first, 16), rows),
                       pl.ds(pl.multiple_of(c * HALF, HALF), HALF)]

    def first_to(d):
        return device(mod(x + d * (1 - c), NX), mod(y + d * c, NY), z, c)

    def second_to(d):
        return device(mod(x + d * c, NX), mod(y + d * (1 - c), NY), z, c)

    sibling = device(x, y, z, 1 - c)
    spot_own = pltpu.make_async_copy(blk, spot(0, 0), local.at[0])
    spot_own.start()
    for d, k in ((1, 0), (-1, 1)):
        copies.send(blk, spot(0, 0), frecv.at[k], first_to(d))
    for d, k in ((1, 0), (-1, 1)):
        copies.send(blk, spot(0, 0), srecv.at[0, k], second_to(d))
    copies.send(blk, spot(0, 0), sibrecv, sibling)

    wait_recv(cz.at[pl.ds(0, NZ - 1)], crecv.at[0])
    cy[0] = jnp.sum(cz[...], axis=0)
    for d in range(1, NX):
        copies.send(cy.at[0], cx.at[x], crecv.at[1], xs[d - 1])

    for k, df in ((0, -1), (1, 1)):
        wait_recv(spot(df, 0), frecv.at[k])
        copies.send(spot(df, 0, k), spot(df, 0, k), frecv.at[2 + k], first_to(-df))
        for d, j in ((1, 0), (-1, 1)):
            copies.send(spot(df, 0), spot(df, 0), srecv.at[1 + k, j], second_to(d))
        copies.send(spot(df, 0), spot(df, 0), sibrecv, sibling)

    wait_recv(cx.at[pl.ds(0, NX - 1)], crecv.at[1])
    got = cy[0]
    for d in range(1, NX):
        got = got + cx[mod(x + d, NX)]
    cy[1] = got
    me = y * NC + c
    for to in dps:
        copies.send(cy.at[1], cd.at[me], crecv.at[2], to)

    def relay(row, df):
        for k, ds in ((0, -1), (1, 1)):
            wait_recv(spot(df, ds), srecv.at[row, k])
            copies.send(spot(df, ds, k), spot(df, ds, k), srecv.at[row, 2 + k], second_to(-ds))
            copies.send(spot(df, ds), spot(df, ds), sibrecv, sibling)

    relay(0, 0)
    for k in (0, 1):
        wait_recv(spot(2, 0, k), frecv.at[2 + k])
    for d, j in ((1, 0), (-1, 1)):
        copies.send(spot(2, 0), spot(2, 0), srecv.at[3, j], second_to(d))
    copies.send(spot(2, 0), spot(2, 0), sibrecv, sibling)
    relay(1, -1)
    relay(2, 1)
    relay(3, 2)
    for row, df in ((0, 0), (1, -1), (2, 1), (3, 2)):
        for k in (0, 1):
            wait_recv(spot(df, 2, k), srecv.at[row, 2 + k])
        copies.send(spot(df, 2), spot(df, 2), sibrecv, sibling)
    wait_recv(cd.at[pl.ds(0, NY * NC - 1)], crecv.at[2])
    got = cy[1]
    for d in range(1, NY * NC):
        got = got + cd[mod(me + d, NY * NC)]
    total[...] = got
    spot_own.wait()
    other = full.at[:, :, pl.ds(pl.multiple_of((1 - c) * HALF, HALF), HALF)]
    wait_recv(other, sibrecv)
    copies.drain()


def gather(wq, wk, wv, wo, cnt):
    vm = pl.BlockSpec(memory_space=pltpu.VMEM)
    hbm = pl.BlockSpec(memory_space=pl.ANY)
    dma = pltpu.SemaphoreType.DMA
    return pl.pallas_call(
        gather_kernel,
        name="gather_weights",
        out_shape=(jax.ShapeDtypeStruct((4, D, D), BF), jax.ShapeDtypeStruct((1, 128), F32)),
        in_specs=[hbm] * 4 + [vm],
        out_specs=(vm, vm),
        scratch_shapes=[
            pltpu.VMEM((4, SHARD, D), BF),
            pltpu.VMEM((NZ, SHARD, HALF), BF),
            pltpu.VMEM((NZ, 1, 128), F32),
            pltpu.VMEM((NX, 1, 128), F32),
            pltpu.VMEM((NY * NC, 1, 128), F32),
            pltpu.VMEM((2, 1, 128), F32),
            pltpu.VMEM((SLAB, HALF), F32),
            pltpu.VMEM((SLAB, HALF), BF),
            dma((4,)), dma, dma((3,)), dma((4,)), dma((4, 4)), dma, dma((96,)),
        ],
        compiler_params=pltpu.CompilerParams(collective_id=0, has_side_effects=True),
    )(wq, wk, wv, wo, cnt)


def reduce_kernel(part, scale, out, ra, rb, rc, rd, re, rf, ta, tb, tf, tz, rz, own, oz,
                  xrecv, zrecv, orecv, arecv, send_sems):
    x, y, z, c = place()
    zs = [device(x, y, mod(z + d, NZ), c) for d in range(1, NZ)]
    right, left = device(mod(x + 1, NX), y, z, c), device(mod(x - 1, NX), y, z, c)
    xr, xl, xo = mod(x + 1, NX), mod(x - 1, NX), mod(x + 2, NX)
    greet(zs + [right, left])
    copies = Copies(send_sems)
    low, high = pl.ds(0, HPX), pl.ds(HPX, HPX)
    copies.send(part.at[xo, low], ra, xrecv.at[0], right)
    copies.send(part.at[xo, high], rb, xrecv.at[1], left)
    copies.send(part.at[xr, high], rc, xrecv.at[2], right)
    copies.send(part.at[xl, low], rd, xrecv.at[3], left)
    wait_recv(ra, xrecv.at[0])
    ta[...] = (part[xr, 0:HPX].astype(F32) + ra[...].astype(F32)).astype(BF)
    copies.send(ta, re, xrecv.at[4], right)
    wait_recv(rb, xrecv.at[1])
    tb[...] = (part[xl, HPX:2 * HPX].astype(F32) + rb[...].astype(F32)).astype(BF)
    copies.send(tb, rf, xrecv.at[5], left)
    wait_recv(rc, xrecv.at[2])
    wait_recv(rd, xrecv.at[3])
    wait_recv(re, xrecv.at[4])
    wait_recv(rf, xrecv.at[5])
    for h in range(HPX):
        low_sum = part[x, h].astype(F32) + rd[h].astype(F32) + re[h].astype(F32)
        high_sum = part[x, HPX + h].astype(F32) + rc[h].astype(F32) + rf[h].astype(F32)
        tf[:, IPZ * h:IPZ * (h + 1), :] = low_sum.reshape(NZ, IPZ, COLS)
        tf[:, IPZ * (HPX + h):IPZ * (HPX + h + 1), :] = high_sum.reshape(NZ, IPZ, COLS)
    tz[...] = tf[...].astype(BF)
    far = sorted(range(1, NZ), key=lambda d: -min(d, NZ - d))
    for d in far:
        copies.send(tz.at[mod(z + d, NZ)], rz.at[z], zrecv, zs[d - 1])
    wait_recv(rz.at[pl.ds(0, NZ - 1)], zrecv)
    acc = tf[z]
    for d in range(1, NZ):
        acc = acc + rz[mod(z + d, NZ)].astype(F32)
    half = HPX * IPZ
    s = scale[...]
    logits = acc[0:half] * s
    grads = acc[half:2 * half]
    top = jnp.max(logits, axis=-1, keepdims=True)
    expo = jnp.exp(logits - top)
    probs = expo / jnp.sum(expo, axis=-1, keepdims=True)
    glog = probs * (grads - jnp.sum(probs * grads, axis=-1, keepdims=True)) * s
    own[...] = jnp.concatenate([probs, glog], axis=0).astype(BF)
    for d in far:
        copies.send(own, oz.at[z], orecv, zs[d - 1])
    keep = pltpu.make_async_copy(own, oz.at[z], arecv.at[4])
    keep.start()
    keep.wait()
    wait_recv(oz.at[pl.ds(0, NZ - 1)], orecv)
    got = oz[...].astype(F32)
    for k in range(2 * HPX):
        out[x, k] = got[:, IPZ * k:IPZ * (k + 1), :].reshape(COLS, COLS).astype(BF)
    copies.send(out.at[x], out.at[x], arecv.at[0], right)
    copies.send(out.at[x], out.at[x], arecv.at[1], left)
    wait_recv(out.at[xl], arecv.at[0])
    copies.send(out.at[xl, low], out.at[xl, low], arecv.at[2], right)
    wait_recv(out.at[xr], arecv.at[1])
    copies.send(out.at[xr, high], out.at[xr, high], arecv.at[3], left)
    wait_recv(out.at[xo, low], arecv.at[2])
    wait_recv(out.at[xo, high], arecv.at[3])
    copies.drain()


def reduce_scatter_gather(part, scale):
    vm = pl.BlockSpec(memory_space=pltpu.VMEM)
    dma = pltpu.SemaphoreType.DMA
    quarter = pltpu.VMEM((HPX, COLS, COLS), BF)
    return pl.pallas_call(
        reduce_kernel,
        name="reduce_probs",
        out_shape=jax.ShapeDtypeStruct((NX, 2 * HPX, COLS, COLS), BF),
        in_specs=[vm, vm],
        out_specs=vm,
        scratch_shapes=[quarter] * 8 + [
            pltpu.VMEM((NZ, CHUNK, COLS), F32),
            pltpu.VMEM((NZ, CHUNK, COLS), BF),
            pltpu.VMEM((NZ, CHUNK, COLS), BF),
            pltpu.VMEM((CHUNK, COLS), BF),
            pltpu.VMEM((NZ, CHUNK, COLS), BF),
            dma((6,)), dma, dma, dma((5,)), dma((48,)),
        ],
        compiler_params=pltpu.CompilerParams(collective_id=1, has_side_effects=True),
    )(part, scale)


def nt(a, b):
    return lax.dot_general(a, b, (((1,), (1,)), ((), ())), preferred_element_type=F32)


def tn(a, b):
    return lax.dot_general(a, b, (((0,), (0,)), ((), ())), preferred_element_type=F32)


def nn(a, b):
    return lax.dot_general(a, b, (((1,), (0,)), ((), ())), preferred_element_type=F32)


def columns_of(masked):
    out = []
    for r in range(2):
        wide = jnp.broadcast_to(masked[r:r + 1, :], (COLS, COLS))
        out.append(jnp.transpose(wide)[:, 0:1])
    return jnp.concatenate(out, axis=0)


def normalize(hidden):
    widened = hidden.astype(F32)
    average = jnp.mean(widened, axis=-1, keepdims=True)
    centred = widened - average
    variance = jnp.mean(centred * centred, axis=-1, keepdims=True)
    inv_std = lax.rsqrt(variance + EPS)
    return widened, centred * inv_std, inv_std


def by_row(alive):
    rows = lax.broadcasted_iota(jnp.int32, (2 * COLS, 1), 0)
    return jnp.where(rows < COLS, alive[0], alive[1])


def lane_low(shape):
    lane = lax.broadcasted_iota(jnp.int32, shape, len(shape) - 1)
    return lax.rem(lane, 2 * HEAD) < HEAD


HEAD = D // HEADS
PAIR = 2 * HEAD


def side(ref, p):
    return jnp.concatenate(
        [ref[0:COLS, PAIR * p:PAIR * (p + 1)], ref[COLS:2 * COLS, PAIR * p:PAIR * (p + 1)]], axis=1)


def stacked(ref, p, low):
    both = side(ref, p)
    zero = jnp.zeros_like(both)
    return jnp.concatenate([jnp.where(low, both, zero), jnp.where(low, zero, both)], axis=0)


def before_kernel(alive, hidden, masked, cot, gain, full, part, q, k, v, ga):
    widened, x_hat, inv_std = normalize(hidden[...])
    normed = (x_hat * gain[...]).astype(BF)
    live = by_row(alive)
    q[...] = (nn(normed, full[0]).astype(BF).astype(F32) * live).astype(BF)
    k[...] = nn(normed, full[1]).astype(BF)
    v[...] = nn(normed, full[2]).astype(BF)
    weight = columns_of(masked[...].astype(F32)) * live
    gm = (cot[...].astype(F32) * weight).astype(BF)
    ga[...] = nt(gm, full[3]).astype(BF)
    low = lane_low((COLS, 2 * PAIR))
    for p in range(HEADS // 2):
        for base, left, right in ((0, q, k), (HPX, ga, v)):
            both = nt(stacked(left, p, low), side(right, p)).astype(BF)
            for j in range(2):
                h = 2 * p + j
                part[h // HPX, base + h % HPX] = both[COLS * j:COLS * (j + 1)]


def before(alive, hidden, masked, cot, gain, full):
    vm = pl.BlockSpec(memory_space=pltpu.VMEM)
    tokens = jax.ShapeDtypeStruct((2 * COLS, D), BF)
    return pl.pallas_call(
        before_kernel,
        name="before",
        out_shape=(jax.ShapeDtypeStruct((NX, 2 * HPX, COLS, COLS), BF), tokens, tokens, tokens, tokens),
        in_specs=[pl.BlockSpec(memory_space=pltpu.SMEM)] + [vm] * 5,
        out_specs=(vm,) * 5,
    )(alive, hidden, masked, cot, gain, full)


def after_kernel(alive, hidden, masked, cot, gain, full, total, soft, q, k, v, ga, mixed, grad,
                 att, gq, gk, gv):
    live = by_row(alive)
    low = lane_low((COLS, 2 * PAIR))
    for p in range(HEADS // 2):
        h0, h1 = 2 * p, 2 * p + 1
        p0, p1 = soft[h0 // HPX, h0 % HPX], soft[h1 // HPX, h1 % HPX]
        g0, g1 = soft[h0 // HPX, HPX + h0 % HPX], soft[h1 // HPX, HPX + h1 % HPX]
        p_side, p_stack = jnp.concatenate([p0, p1], axis=1), jnp.concatenate([p0, p1], axis=0)
        g_side, g_stack = jnp.concatenate([g0, g1], axis=1), jnp.concatenate([g0, g1], axis=0)
        for dst, value in ((att, nn(p_side, stacked(v, p, low))), (gv, tn(p_stack, stacked(ga, p, low))),
                           (gq, nn(g_side, stacked(k, p, low))), (gk, tn(g_stack, stacked(q, p, low)))):
            value = value.astype(BF)
            dst[0:COLS, PAIR * p:PAIR * (p + 1)] = value[:, 0:PAIR]
            dst[COLS:2 * COLS, PAIR * p:PAIR * (p + 1)] = value[:, PAIR:2 * PAIR]
    widened, x_hat, inv_std = normalize(hidden[...])
    mixed[...] = (widened + live * nn(att[...], full[3])).astype(BF)
    gn = nt(gq[...], full[0]) * live + nt(gk[...], full[1]) + nt(gv[...], full[2])
    scaled = gn * gain[...]
    grad_x = inv_std * (scaled - jnp.mean(scaled, axis=-1, keepdims=True)
                        - x_hat * jnp.mean(scaled * x_hat, axis=-1, keepdims=True))
    ratio = total[0:1, 1:2] * COLS / jnp.maximum(total[0:1, 0:1], 1.0)
    weight = columns_of(masked[...].astype(F32)) * live
    grad[...] = (ratio * (cot[...].astype(F32) * weight + grad_x)).astype(BF)


def after(alive, hidden, masked, cot, gain, full, total, soft, q, k, v, ga):
    vm = pl.BlockSpec(memory_space=pltpu.VMEM)
    tokens = jax.ShapeDtypeStruct((2 * COLS, D), BF)
    return pl.pallas_call(
        after_kernel,
        name="after",
        out_shape=(tokens, tokens),
        in_specs=[pl.BlockSpec(memory_space=pltpu.SMEM)] + [vm] * 11,
        out_specs=(vm, vm),
        scratch_shapes=[pltpu.VMEM((2 * COLS, D), BF)] * 4,
    )(alive, hidden, masked, cot, gain, full, total, soft, q, k, v, ga)


def body(hidden, masked, depths, norm_gain, w_query, w_key, w_value, w_out, cotangent):
    shape = hidden.shape
    first_row = lax.axis_index("row") * shape[1]
    alive = (first_row + jnp.arange(2, dtype=jnp.int32) < depths[0]).astype(F32)
    masks = masked[0]
    counted = jnp.sum(masks.astype(F32) * alive[:, None])
    lane = jnp.arange(128)
    cnt = jnp.where(lane == 0, counted, jnp.where(lane == 1, jnp.sum(alive), 0.0)).reshape(1, 128)
    scale = jnp.broadcast_to(1.0 / jnp.sqrt(depths[0].astype(F32) * HEAD), (1, 128))
    tokens = (shape[1] * shape[2], shape[3])
    hid, cot = hidden.reshape(tokens), cotangent.reshape(tokens)
    gain = norm_gain.reshape(1, D)
    full, total = gather(w_query, w_key, w_value, w_out, cnt)
    part, q, k, v, ga = before(alive, hid, masks, cot, gain, full)
    soft = reduce_scatter_gather(part, scale)
    mixed, grad = after(alive, hid, masks, cot, gain, full, total, soft, q, k, v, ga)
    return mixed.reshape(shape), grad.reshape(shape)


def solution(mesh):
    return jax.shard_map(
        body,
        mesh=mesh,
        in_specs=(
            P("dp", "row", None, None),
            P("dp", "row", None),
            P("dp"),
            P(),
            P("row", None),
            P("row", None),
            P("row", None),
            P("row", None),
            P("dp", "row", None, None),
        ),
        out_specs=(P("dp", "row", None, None), P("dp", "row", None, None)),
        check_vma=False,
    )
```

time: 915 us -> 118 us (0.13); the launches traced: 904 us -> 117 us
  waiting for transfers between devices: 696 us -> 0 us
  blocking collectives: 112 us -> 0 us
  Pallas kernels: 0 us -> 110 us
  matrix products: 44 us -> 0 us
  local copies, waits for them, and re-layouts: 24.6 us -> 1.87 us
  between operations: 16.6 us -> 1.35 us
    all_gather x4 -> x0, waiting for transfers between devices: 418 us -> none  [the longest x1 136 us: body(): lax.all_gather(w_query, 'row', axis=0, tiled=True)]
    psum x1 -> x0, waiting for transfers between devices: 275 us -> none  [body(): logits = lax.psum(partial_value, 'row') * scale]
    psum x1 -> x0, blocking collectives: 112 us -> none  [body(): lax.psum((jnp.sum(alive) * columns, jnp.sum(weighting)), ('dp', 'row'))]
    pallas_call x0 -> x4, Pallas kernels: none -> 110 us  [the longest x1 50.5 us: gather(): pl.pallas_call(gather_kernel, name='gather_weights', out_shape=(jax.Shape...]
    dot_general x14 -> x0, matrix products: 44 us -> none  [the longest x1 10.9 us: body(): jnp.einsum('hij,rihe->rjhe', grad_logits, query_live, preferred_element_t...]
    unnamed x32 -> x2, local copies, waits for them, and re-layouts: 11.4 us -> 0.01 us
  transfers between devices with their start and end apart: 5 -> 0, of which waited for: 5 -> 0; matrix products, arithmetic and copies ran while one was open for 2% -> 0% of each run, Pallas kernels for 0% -> 0%
where the time goes in v1:
time: 118 us; the launch traced here: 117 us
  Pallas kernels  110 us (93%)
  other arithmetic  3.73 us (3%)
  local copies, waits for them, and re-layouts  1.87 us (2%)
  between operations  1.35 us (1%)
    pallas_call x1, Pallas kernels, gather(): pl.pallas_call(gather_kernel, name='gather_weights', out_shape=(jax.Shape...  50.5 us
    pallas_call x1, Pallas kernels, reduce_scatter_gather(): pl.pallas_call(reduce_kernel, name='reduce_probs', out_shape=jax.ShapeDty...  47.5 us
    pallas_call x1, Pallas kernels, after(): pl.pallas_call(after_kernel, name='after', out_shape=(tokens, tokens), in...  6.13 us
    pallas_call x1, Pallas kernels, before(): pl.pallas_call(before_kernel, name='before', out_shape=(jax.ShapeDtypeStr...  5.58 us

profile of v1, /device:TPU:1, one launch (start us, length us, event | category | flops | bytes accessed | tf_op | source)
XLA Modules:
  0.0 116.7 jit_solution(4804965505236390543)
XLA Ops:
  1.3 0.6 broadcast_in_dim.19.scale
  1.9 0.6 fusion
  2.5 0.0 copy-start
  2.5 1.4 %multiply_reduce_fusion = f32[]{:T(128)} fusion(f32[2]{0:T(128)S(1)} %get-tuple-element.21.alive, s32[1,2,128]{2,1,0:T(2,128)} %param.10), kind=kLoop, calls=%fused_computation.3 | loop fusion | flops 767 | bytes 1036 | tf_op jit(solution)/shard_map/reduce_sum | solution.py:408
  3.9 1.8 %compare_select_fusion.1.cnt = f32[1,128]{1,0:T(1,128)} fusion(f32[]{:T(128)} %get-tuple-element.20, f32[]{:T(128)} %multiply_reduce_fusion), kind=kLoop, calls=%fused_computation.1 | loop fusion | flops 512 | bytes 520 | tf_op jit(solution)/shard_map/jit(_where)/select_n | solution.py:410
  5.6 1.3 %reshape.47.gain = f32[1,768]{1,0:T(1,128)} reshape(f32[768]{0:T(1024)} %param.12) | data formatting | bytes 6144 | tf_op jit(solution)/shard_map/reshape | solution.py:414
  6.9 50.5 %gather_weights.1 = (bf16[4,768,768]{2,1,0:T(8,128)(2,1)}, f32[1,128]{1,0:T(1,128)}) custom-call(bf16[12,768]{1,0:T(8,128)(2,1)} %wq.1, bf16[12,768]{1,0:T(8,128)(2,1)} %wk.1, bf16[12,768]{1,0:T(8,128)(2,1)} %wv.1, bf16[12,768]{1,0:T(8,128)(2,1)} %wo.1, f32[1,128]{1,0:T(1,128)} %compare_select_fusion.1.cnt), custom_call_target="tpu_custom_call" | custom-call | tf_op jit(solution)/shard_map/gather_weights/pallas_call | solution.py:171
  57.5 0.0 copy-done
  57.5 5.6 %before.1 = (bf16[4,6,128,128]{3,2,1,0:T(8,128)(2,1)}, bf16[256,768]{1,0:T(8,128)(2,1)}, bf16[256,768]{1,0:T(8,128)(2,1)}, bf16[256,768]{1,0:T(8,128)(2,1)}, bf16[256,768]{1,0:T(8,128)(2,1)}) custom-call(f32[2]{0:T(128)} %copy-done, bf16[256,768]{1,0:T(8,128)(2,1)} %bitcast.9, s32[2,128]{1,0:T(2,128)} %bitcast.13, bf16[256,768]{1,0:T(8,128)(2,1)} %bitcast.11, ...), custom_call_target="tpu_custom_call" | custom-call | tf_op jit(solution)/shard_map/before/pallas_call | solution.py:355
  63.1 47.5 %reduce_probs.1.soft = bf16[4,6,128,128]{3,2,1,0:T(8,128)(2,1)} custom-call(bf16[4,6,128,128]{3,2,1,0:T(8,128)(2,1)} %get-tuple-element.13.part, f32[1,128]{1,0:T(1,128)} %broadcast_in_dim.19.scale), custom_call_target="tpu_custom_call" | custom-call | tf_op jit(solution)/shard_map/reduce_probs/pallas_call | solution.py:261
  110.5 6.1 %after.1 = (bf16[256,768]{1,0:T(8,128)(2,1)}, bf16[256,768]{1,0:T(8,128)(2,1)}) custom-call(f32[2]{0:T(128)} %copy-done, bf16[256,768]{1,0:T(8,128)(2,1)} %bitcast.10, s32[2,128]{1,0:T(2,128)} %bitcast.14, bf16[256,768]{1,0:T(8,128)(2,1)} %bitcast.12, f32[1,768]{1,0:T(1,128)} %reshape.47.gain, bf16[4,768,768]{2,1,0:T(8,128)(2,1)} %get-tuple-element.11.full, ...), custom_call_target="tpu_custom_call" | custom-call | tf_op jit(solution)/shard_map/after/pallas_call | solution.py:393
Async XLA Ops:
  2.5 55.0 %copy-start = (f32[2]{0:T(128)}, f32[2]{0:T(128)S(1)}, u32[]{:S(2)}) copy-start(f32[2]{0:T(128)S(1)} %get-tuple-element.21.alive) | copy-start | bytes 28

commit v2 on v0

v2 whole, which is shorter than its diff:
```python
import jax
import jax.numpy as jnp
from jax import lax
from jax.experimental import pallas as pl
from jax.experimental.pallas import tpu as pltpu
from jax.sharding import PartitionSpec as P

HEADS = 12
EPS = 1e-05
NX, NY, NZ, NC = 4, 4, 16, 2
D = 768
COLS = 128
SHARD = D // (NX * NZ)
SLAB = SHARD * NZ
HALF = D // NC
HPX = HEADS // NX
IPZ = COLS // NZ
CHUNK = HPX * IPZ
HEAD = D // HEADS
PAIR = 2 * HEAD
MESH = pl.DeviceIdType.MESH
BF, F32 = jnp.bfloat16, jnp.float32


def place():
    dp, row = lax.axis_index("dp"), lax.axis_index("row")
    return lax.div(row, NZ), lax.div(dp, NC), lax.rem(row, NZ), lax.rem(dp, NC)


def device(x, y, z, c):
    return (y * NC + c, x * NZ + z)


def mod(a, n):
    return lax.rem(a + n, n)


class Copies:
    def __init__(self, sems, group_sems):
        self.sems, self.sent = sems, []
        self.group_sems, self.groups = group_sems, []

    def spread(self, sources, dst, recv, devices, all_of):
        sem = self.group_sems.at[len(self.groups)]
        for src, to in zip(sources, devices, strict=True):
            pltpu.make_async_remote_copy(
                src_ref=src, dst_ref=dst, send_sem=sem, recv_sem=recv, device_id=to, device_id_type=MESH).start()
        self.groups.append((all_of, sem))

    def send(self, src, dst, recv, to):
        copy = pltpu.make_async_remote_copy(
            src_ref=src, dst_ref=dst, send_sem=self.sems.at[len(self.sent)], recv_sem=recv,
            device_id=to, device_id_type=MESH)
        copy.start()
        self.sent.append(copy)

    def drain(self):
        for copy in self.sent:
            copy.wait_send()
        for ref, sem in self.groups:
            wait_recv(ref, sem)


def wait_recv(ref, sem):
    pltpu.make_async_copy(ref, ref, sem).wait()


def nt(a, b):
    return lax.dot_general(a, b, (((1,), (1,)), ((), ())), preferred_element_type=F32)


def tn(a, b):
    return lax.dot_general(a, b, (((0,), (0,)), ((), ())), preferred_element_type=F32)


def nn(a, b):
    return lax.dot_general(a, b, (((1,), (0,)), ((), ())), preferred_element_type=F32)


def columns_of(masked):
    out = []
    for r in range(2):
        wide = jnp.broadcast_to(masked[r:r + 1, :], (COLS, COLS))
        out.append(jnp.transpose(wide)[:, 0:1])
    return jnp.concatenate(out, axis=0)


def lane_low(shape):
    lane = lax.broadcasted_iota(jnp.int32, shape, len(shape) - 1)
    return lax.rem(lane, 2 * HEAD) < HEAD


def side(ref, p):
    return jnp.concatenate(
        [ref[0:COLS, PAIR * p:PAIR * (p + 1)], ref[COLS:2 * COLS, PAIR * p:PAIR * (p + 1)]], axis=1)


def stacked(ref, p, low):
    both = side(ref, p)
    zero = jnp.zeros_like(both)
    return jnp.concatenate([jnp.where(low, both, zero), jnp.where(low, zero, both)], axis=0)


def step_kernel(depth, hidden, masked, gain, wq, wk, wv, wo, cot, mixed, grad,
                full, stack, zbuf, cz, cx, cd, cy, tmp, blk, x_hat, inv_std, normed, gm, weight, live,
                q, k, v, ga, att, gq, gk, gv, part, ra, rb, rd, rc, re, rf, ta, tb, tf, tz, rz, own, oz, soft,
                local, zrecv, crecv, frecv, srecv, sibrecv, xrecv, rrecv, orecv, arecv, send_sems, group_sems):
    x, y, z, c = place()
    loads = [pltpu.make_async_copy(w, stack.at[i], local.at[i]) for i, w in enumerate((wq, wk, wv, wo))]
    for load in loads:
        load.start()
    far = sorted(range(1, NZ), key=lambda d: -min(d, NZ - d))
    zs = [device(x, y, mod(z + d, NZ), c) for d in far]
    xs = [device(mod(x + d, NX), y, z, c) for d in range(1, NX)]
    dps = [device(x, lax.div(e, NC), z, lax.rem(e, NC))
           for e in [mod(y * NC + c + d, NY * NC) for d in range(1, NY * NC)]]
    right, left = xs[0], xs[NX - 2]
    barrier = pltpu.get_barrier_semaphore()
    for to in zs + xs + dps:
        pl.semaphore_signal(barrier, inc=1, device_id=to, device_id_type=MESH)

    widened = hidden[...].astype(F32)
    centred = widened - jnp.mean(widened, axis=-1, keepdims=True)
    inv = lax.rsqrt(jnp.mean(centred * centred, axis=-1, keepdims=True) + EPS)
    inv_std[...] = inv
    x_hat[...] = centred * inv
    normed[...] = (centred * inv * gain[...].reshape(1, D)).astype(BF)
    rows = lax.broadcasted_iota(jnp.int32, (2 * COLS, 1), 0)
    alive = ((x * NZ + z) * 2 + lax.div(rows, COLS) < depth[0]).astype(F32)
    live[...] = alive
    token = columns_of(masked[...].astype(F32)) * alive
    weight[...] = token
    gm[...] = (cot[...].astype(F32) * token).astype(BF)
    lane = lax.broadcasted_iota(jnp.int32, (1, 128), 1)
    counted = jnp.sum(token, axis=0, keepdims=True)
    rows_live = jnp.sum(alive, axis=0, keepdims=True)
    cy[2] = jnp.where(lane == 0, counted, jnp.where(lane == 1, rows_live, 0.0))

    for load in loads:
        load.wait()
    pl.semaphore_wait(barrier, NZ - 1 + NX - 1 + NY * NC - 1)

    copies = Copies(send_sems, group_sems)
    mine = stack.at[y, :, pl.ds(pl.multiple_of(c * HALF, HALF), HALF)]
    others = pl.ds(0, NZ - 1)
    copies.spread([mine] * (NZ - 1), zbuf.at[z], zrecv, zs, zbuf.at[others])
    copies.spread([cy.at[2]] * (NZ - 1), cz.at[z], crecv.at[0], zs, cz.at[others])
    keep = pltpu.make_async_copy(mine, zbuf.at[z], local.at[0])
    keep.start()
    keep.wait()
    cz[z] = cy[2]
    wait_recv(zbuf.at[others], zrecv)
    for i in range(NZ):
        tmp[SHARD * i:SHARD * (i + 1), :] = zbuf[i].astype(F32)
    blk[...] = tmp[...].astype(BF)

    def spot(df, ds, piece=None):
        bx = mod(x + df * (1 - c) + ds * c, NX)
        by = mod(y + df * c + ds * (1 - c), NY)
        first, count = (0, SLAB) if piece is None else (piece * (SLAB // 2), SLAB // 2)
        return full.at[by, pl.ds(pl.multiple_of(bx * SLAB + first, 16), count),
                       pl.ds(pl.multiple_of(c * HALF, HALF), HALF)]

    def first_to(d):
        return device(mod(x + d * (1 - c), NX), mod(y + d * c, NY), z, c)

    def second_to(d):
        return device(mod(x + d * c, NX), mod(y + d * (1 - c), NY), z, c)

    sibling = device(x, y, z, 1 - c)
    spot_own = pltpu.make_async_copy(blk, spot(0, 0), local.at[0])
    spot_own.start()
    for d, j in ((1, 0), (-1, 1)):
        copies.send(blk, spot(0, 0), frecv.at[j], first_to(d))
    for d, j in ((1, 0), (-1, 1)):
        copies.send(blk, spot(0, 0), srecv.at[0, j], second_to(d))
    copies.send(blk, spot(0, 0), sibrecv, sibling)

    wait_recv(cz.at[others], crecv.at[0])
    cy[0] = jnp.sum(cz[...], axis=0)
    for to in xs:
        copies.send(cy.at[0], cx.at[x], crecv.at[1], to)

    for i, df in ((0, -1), (1, 1)):
        wait_recv(spot(df, 0), frecv.at[i])
        copies.send(spot(df, 0, i), spot(df, 0, i), frecv.at[2 + i], first_to(-df))
        for d, j in ((1, 0), (-1, 1)):
            copies.send(spot(df, 0), spot(df, 0), srecv.at[1 + i, j], second_to(d))
        copies.send(spot(df, 0), spot(df, 0), sibrecv, sibling)

    wait_recv(cx.at[pl.ds(0, NX - 1)], crecv.at[1])
    got = cy[0]
    for d in range(1, NX):
        got = got + cx[mod(x + d, NX)]
    cy[1] = got
    me = y * NC + c
    for to in dps:
        copies.send(cy.at[1], cd.at[me], crecv.at[2], to)

    def relay(row, df):
        for i, ds in ((0, -1), (1, 1)):
            wait_recv(spot(df, ds), srecv.at[row, i])
            copies.send(spot(df, ds, i), spot(df, ds, i), srecv.at[row, 2 + i], second_to(-ds))
            copies.send(spot(df, ds), spot(df, ds), sibrecv, sibling)

    relay(0, 0)
    for i in (0, 1):
        wait_recv(spot(2, 0, i), frecv.at[2 + i])
    for d, j in ((1, 0), (-1, 1)):
        copies.send(spot(2, 0), spot(2, 0), srecv.at[3, j], second_to(d))
    copies.send(spot(2, 0), spot(2, 0), sibrecv, sibling)
    relay(1, -1)
    relay(2, 1)
    relay(3, 2)
    for row, df in ((0, 0), (1, -1), (2, 1), (3, 2)):
        for i in (0, 1):
            wait_recv(spot(df, 2, i), srecv.at[row, 2 + i])
        copies.send(spot(df, 2), spot(df, 2), sibrecv, sibling)
    spot_own.wait()
    wait_recv(full.at[:, :, pl.ds(pl.multiple_of((1 - c) * HALF, HALF), HALF)], sibrecv)

    xr, xl, xo = mod(x + 1, NX), mod(x - 1, NX), mod(x + 2, NX)
    low = lane_low((COLS, 2 * PAIR))
    logit, slope = 0, 1

    def partial(side_of, with_, kind):
        for p in range(HEADS // 2):
            both = nt(stacked(side_of, p, low), side(with_, p)).astype(BF)
            for j in range(2):
                h = 2 * p + j
                part[kind, h // HPX, h % HPX] = both[COLS * j:COLS * (j + 1)]

    q[...] = (nn(normed[...], full[0]).astype(BF).astype(F32) * live[...]).astype(BF)
    k[...] = nn(normed[...], full[1]).astype(BF)
    partial(q, k, logit)
    copies.send(part.at[logit, xo], ra, xrecv.at[0], right)
    copies.send(part.at[logit, xl], rd, xrecv.at[3], left)
    v[...] = nn(normed[...], full[2]).astype(BF)
    ga[...] = nt(gm[...], full[3]).astype(BF)
    partial(ga, v, slope)
    copies.send(part.at[slope, xo], rb, xrecv.at[1], left)
    copies.send(part.at[slope, xr], rc, xrecv.at[2], right)
    wait_recv(ra, xrecv.at[0])
    ta[...] = (part[logit, xr].astype(F32) + ra[...].astype(F32)).astype(BF)
    copies.send(ta, re, xrecv.at[4], right)
    wait_recv(rb, xrecv.at[1])
    tb[...] = (part[slope, xl].astype(F32) + rb[...].astype(F32)).astype(BF)
    copies.send(tb, rf, xrecv.at[5], left)

    for kind, one, sem_one, two, sem_two in ((logit, rd, 3, re, 4), (slope, rc, 2, rf, 5)):
        wait_recv(one, xrecv.at[sem_one])
        wait_recv(two, xrecv.at[sem_two])
        for h in range(HPX):
            value = part[kind, x, h].astype(F32) + one[h].astype(F32) + two[h].astype(F32)
            tf[kind, :, IPZ * h:IPZ * (h + 1), :] = value.reshape(NZ, IPZ, COLS)
        tz[kind] = tf[kind].astype(BF)
        copies.spread([tz.at[kind, mod(z + d, NZ)] for d in far], rz.at[kind, z], rrecv.at[kind], zs,
                      rz.at[kind, others])

    def over_z(kind):
        wait_recv(rz.at[kind, others], rrecv.at[kind])
        acc = tf[kind, z]
        for d in range(1, NZ):
            acc = acc + rz[kind, mod(z + d, NZ)].astype(F32)
        return acc

    def spread_rows(kind, value):
        own[kind] = value.astype(BF)
        copies.spread([own.at[kind]] * (NZ - 1), oz.at[kind, z], orecv.at[kind], zs, oz.at[kind, others])
        oz[kind, z] = value.astype(BF)

    scale = 1.0 / jnp.sqrt(jnp.full((1, COLS), depth[0], jnp.int32).astype(F32) * HEAD)
    logits = over_z(logit) * scale
    expo = jnp.exp(logits - jnp.max(logits, axis=-1, keepdims=True))
    probs = expo / jnp.sum(expo, axis=-1, keepdims=True)
    spread_rows(logit, probs)
    slopes = over_z(slope)
    spread_rows(slope, probs * (slopes - jnp.sum(probs * slopes, axis=-1, keepdims=True)) * scale)

    for kind in (logit, slope):
        wait_recv(oz.at[kind, others], orecv.at[kind])
        got = oz[kind].astype(F32)
        for h in range(HPX):
            soft[kind, x, h] = got[:, IPZ * h:IPZ * (h + 1), :].reshape(COLS, COLS).astype(BF)
        ahead, behind = (right, left) if kind == logit else (left, right)
        copies.send(soft.at[kind, x], soft.at[kind, x], arecv.at[kind, 0], ahead)
        copies.send(soft.at[kind, x], soft.at[kind, x], arecv.at[kind, 1], behind)

    def collect(kind):
        near = xl if kind == logit else xr
        wait_recv(soft.at[kind, near], arecv.at[kind, 0])
        copies.send(soft.at[kind, near], soft.at[kind, near], arecv.at[kind, 2], right if kind == logit else left)

    def finish(kind):
        wait_recv(soft.at[kind, xr if kind == logit else xl], arecv.at[kind, 1])
        wait_recv(soft.at[kind, xo], arecv.at[kind, 2])

    def apply(kind, across, across_to, down, down_to):
        for p in range(HEADS // 2):
            h0, h1 = 2 * p, 2 * p + 1
            s0, s1 = soft[kind, h0 // HPX, h0 % HPX], soft[kind, h1 // HPX, h1 % HPX]
            for dst, value in (
                    (across_to, nn(jnp.concatenate([s0, s1], axis=1), stacked(across, p, low))),
                    (down_to, tn(jnp.concatenate([s0, s1], axis=0), stacked(down, p, low)))):
                value = value.astype(BF)
                dst[0:COLS, PAIR * p:PAIR * (p + 1)] = value[:, 0:PAIR]
                dst[COLS:2 * COLS, PAIR * p:PAIR * (p + 1)] = value[:, PAIR:2 * PAIR]

    collect(logit)
    collect(slope)
    finish(logit)
    apply(logit, v, att, ga, gv)
    mixed[...] = (hidden[...].astype(F32) + live[...] * nn(att[...], full[3])).astype(BF)
    acc = nt(gv[...], full[2])
    finish(slope)
    apply(slope, k, gq, q, gk)
    acc = acc + nt(gq[...], full[0]) * live[...] + nt(gk[...], full[1])
    scaled = acc * gain[...].reshape(1, D)
    hat = x_hat[...]
    grad_x = inv_std[...] * (scaled - jnp.mean(scaled, axis=-1, keepdims=True)
                             - hat * jnp.mean(scaled * hat, axis=-1, keepdims=True))
    wait_recv(cd.at[pl.ds(0, NY * NC - 1)], crecv.at[2])
    total = cy[1]
    for d in range(1, NY * NC):
        total = total + cd[mod(me + d, NY * NC)]
    ratio = total[:, 1:2] / jnp.maximum(total[:, 0:1], 1.0)
    grad[...] = (ratio * (cot[...].astype(F32) * weight[...] + grad_x)).astype(BF)
    copies.drain()


def step(depths, hidden, masked, gain, wq, wk, wv, wo, cot):
    vm = pl.BlockSpec(memory_space=pltpu.VMEM)
    hbm = pl.BlockSpec(memory_space=pl.ANY)
    dma = pltpu.SemaphoreType.DMA
    tokens = jax.ShapeDtypeStruct((2 * COLS, D), BF)
    act, col = pltpu.VMEM((2 * COLS, D), BF), pltpu.VMEM((2 * COLS, 1), F32)
    quarter = pltpu.VMEM((HPX, COLS, COLS), BF)
    chunks = pltpu.VMEM((2, NZ, CHUNK, COLS), BF)
    heads = pltpu.VMEM((2, NX, HPX, COLS, COLS), BF)
    return pl.pallas_call(
        step_kernel,
        name="step",
        out_shape=(tokens, tokens),
        in_specs=[pl.BlockSpec(memory_space=pltpu.SMEM), vm, vm, vm] + [hbm] * 4 + [vm],
        out_specs=(vm, vm),
        scratch_shapes=[
            pltpu.VMEM((4, D, D), BF),
            pltpu.VMEM((4, SHARD, D), BF),
            pltpu.VMEM((NZ, SHARD, HALF), BF),
            pltpu.VMEM((NZ, 1, 128), F32),
            pltpu.VMEM((NX, 1, 128), F32),
            pltpu.VMEM((NY * NC, 1, 128), F32),
            pltpu.VMEM((3, 1, 128), F32),
            pltpu.VMEM((SLAB, HALF), F32),
            pltpu.VMEM((SLAB, HALF), BF),
            pltpu.VMEM((2 * COLS, D), F32), col, act, act, col, col,
            act, act, act, act, act, act, act, act,
            heads, quarter, quarter, quarter, quarter, quarter, quarter, quarter, quarter,
            pltpu.VMEM((2, NZ, CHUNK, COLS), F32), chunks, chunks, pltpu.VMEM((2, CHUNK, COLS), BF), chunks, heads,
            dma((4,)), dma, dma((3,)), dma((4,)), dma((4, 4)), dma, dma((6,)), dma((2,)), dma((2,)), dma((2, 3)),
            dma((80,)), dma((6,)),
        ],
        compiler_params=pltpu.CompilerParams(collective_id=0, has_side_effects=True),
    )(depths, hidden, masked, gain, wq, wk, wv, wo, cot)


def body(hidden, masked, depths, norm_gain, w_query, w_key, w_value, w_out, cotangent):
    shape = hidden.shape
    tokens = (shape[1] * shape[2], shape[3])
    mixed, grad = step(depths, hidden.reshape(tokens), masked[0], norm_gain, w_query, w_key, w_value, w_out,
                       cotangent.reshape(tokens))
    return mixed.reshape(shape), grad.reshape(shape)


def solution(mesh):
    return jax.shard_map(
        body,
        mesh=mesh,
        in_specs=(
            P("dp", "row", None, None),
            P("dp", "row", None),
            P("dp"),
            P(),
            P("row", None),
            P("row", None),
            P("row", None),
            P("row", None),
            P("dp", "row", None, None),
        ),
        out_specs=(P("dp", "row", None, None), P("dp", "row", None, None)),
        check_vma=False,
    )
```

time: 915 us -> 94.2 us (0.10); the launches traced: 904 us -> 92.7 us
  waiting for transfers between devices: 696 us -> 0 us
  blocking collectives: 112 us -> 0 us
  Pallas kernels: 0 us -> 88.9 us
  matrix products: 44 us -> 0 us
  local copies, waits for them, and re-layouts: 24.6 us -> 2.57 us
  between operations: 16.6 us -> 1.3 us
  other arithmetic: 11.4 us -> 0 us
    all_gather x4 -> x0, waiting for transfers between devices: 418 us -> none  [the longest x1 136 us: body(): lax.all_gather(w_query, 'row', axis=0, tiled=True)]
    psum x1 -> x0, waiting for transfers between devices: 275 us -> none  [body(): logits = lax.psum(partial_value, 'row') * scale]
    psum x1 -> x0, blocking collectives: 112 us -> none  [body(): lax.psum((jnp.sum(alive) * columns, jnp.sum(weighting)), ('dp', 'row'))]
    pallas_call x0 -> x1, Pallas kernels: none -> 88.9 us  [step(): pl.pallas_call(step_kernel, name='step', out_shape=(tokens, tokens), in_s...]
    dot_general x14 -> x0, matrix products: 44 us -> none  [the longest x1 10.9 us: body(): jnp.einsum('hij,rihe->rjhe', grad_logits, query_live, preferred_element_t...]
  transfers between devices with their start and end apart: 5 -> 0, of which waited for: 5 -> 0; matrix products, arithmetic and copies ran while one was open for 2% -> 0% of each run, Pallas kernels for 0% -> 0%
where the time goes in v2:
time: 94.2 us; the launch traced here: 92.7 us
  Pallas kernels  88.9 us (94%)
  local copies, waits for them, and re-layouts  2.57 us (3%)
  between operations  1.3 us (1%)
    pallas_call x1, Pallas kernels, step(): pl.pallas_call(step_kernel, name='step', out_shape=(tokens, tokens), in_s...  88.9 us
    unnamed x4, local copies, waits for them, and re-layouts  2.57 us

profile of v2, /device:TPU:1, one launch (start us, length us, event | category | flops | bytes accessed | tf_op | source)
XLA Modules:
  0.0 92.7 jit_solution(10032865266855739104)
XLA Ops:
  1.3 88.9 %step.1 = (bf16[256,768]{1,0:T(8,128)(2,1)}, bf16[256,768]{1,0:T(8,128)(2,1)}) custom-call(s32[1]{0:T(128)S(6)} %copy.13.depth, bf16[256,768]{1,0:T(8,128)(2,1)} %bitcast.7, s32[2,128]{1,0:T(2,128)} %bitcast.9, f32[768]{0:T(1024)} %gain.1, bf16[12,768]{1,0:T(8,128)(2,1)} %wq.1, bf16[12,768]{1,0:T(8,128)(2,1)} %wk.1, bf16[12,768]{1,0:T(8,128)(2,1)} %wv.1, ...), custom_call_target="tpu_custom_call" | custom-call | tf_op jit(solution)/shard_map/step/pallas_call | solution.py:340
  90.1 0.0 copy-start
  90.2 1.8 %copy.14 = bf16[1,2,128,768]{3,2,1,0:T(8,128)(2,1)} copy(bf16[1,2,128,768]{3,2,1,0:T(8,128)(2,1)} %bitcast.6) | data formatting | bytes 786432
  92.0 0.0 copy-done
  92.0 0.7 copy.15
Async XLA Ops:
  90.1 1.8 %copy-start = (bf16[256,768]{1,0:T(8,128)(2,1)S(1)}, bf16[256,768]{1,0:T(8,128)(2,1)}, u32[]{:S(2)}) copy-start(bf16[256,768]{1,0:T(8,128)(2,1)} %get-tuple-element.5) | copy-start | bytes 1179652

commit v3 on v2

--- a/solution.py
+++ b/solution.py
@@ -103,7 +103,7 @@
 
 def step_kernel(depth, hidden, masked, gain, wq, wk, wv, wo, cot, mixed, grad,
                 full, stack, zbuf, cz, cx, cd, cy, tmp, blk, x_hat, inv_std, normed, gm, weight, live,
-                q, k, v, ga, att, gq, gk, gv, part, ra, rb, rd, rc, re, rf, ta, tb, tf, tz, rz, own, oz, soft,
+                q, k, v, ga, att, gq, gk, gv, part, rx, tf, tz, rz, own, oz, soft,
                 local, zrecv, crecv, frecv, srecv, sibrecv, xrecv, rrecv, orecv, arecv, send_sems, group_sems):
     x, y, z, c = place()
     loads = [pltpu.make_async_copy(w, stack.at[i], local.at[i]) for i, w in enumerate((wq, wk, wv, wo))]
@@ -111,13 +111,35 @@
         load.start()
     far = sorted(range(1, NZ), key=lambda d: -min(d, NZ - d))
     zs = [device(x, y, mod(z + d, NZ), c) for d in far]
-    xs = [device(mod(x + d, NX), y, z, c) for d in range(1, NX)]
+    xs = [device(mod(x + d, NX), y, z, c) for d in (2, 1, 3)]
     dps = [device(x, lax.div(e, NC), z, lax.rem(e, NC))
            for e in [mod(y * NC + c + d, NY * NC) for d in range(1, NY * NC)]]
-    right, left = xs[0], xs[NX - 2]
+    def along(d):
+        return device(x, y, mod(z + d, NZ), c)
+
+    reach = NZ // 4
+    steps = [d * e for d in range(reach, 0, -1) for e in (1, -1)]
+    near = [along(d) for d in steps]
     barrier = pltpu.get_barrier_semaphore()
-    for to in zs + xs + dps:
+    for to in near + xs + dps:
         pl.semaphore_signal(barrier, inc=1, device_id=to, device_id_type=MESH)
+
+    for load in loads:
+        load.wait()
+    pl.semaphore_wait(barrier, 2 * reach + NX - 1 + NY * NC - 1)
+
+    copies = Copies(send_sems, group_sems)
+    mine = stack.at[y, :, pl.ds(pl.multiple_of(c * HALF, HALF), HALF)]
+    others = pl.ds(0, NZ - 1)
+    for d, to in zip(steps, near, strict=True):
+        copies.send(mine, zbuf.at[z], zrecv.at[0 if abs(d) < reach else 1 if d > 0 else 2], to)
+    keep = pltpu.make_async_copy(mine, zbuf.at[z], local.at[0])
+    keep.start()
+    for sign, sem in ((1, 1), (-1, 2)):
+        came = zbuf.at[mod(z - sign * reach, NZ)]
+        wait_recv(came, zrecv.at[sem])
+        for d in range(reach if sign > 0 else reach - 1, 0, -1):
+            copies.send(came, came, zrecv.at[3], along(sign * d))
 
     widened = hidden[...].astype(F32)
     centred = widened - jnp.mean(widened, axis=-1, keepdims=True)
@@ -135,21 +157,10 @@
     counted = jnp.sum(token, axis=0, keepdims=True)
     rows_live = jnp.sum(alive, axis=0, keepdims=True)
     cy[2] = jnp.where(lane == 0, counted, jnp.where(lane == 1, rows_live, 0.0))
-
-    for load in loads:
-        load.wait()
-    pl.semaphore_wait(barrier, NZ - 1 + NX - 1 + NY * NC - 1)
-
-    copies = Copies(send_sems, group_sems)
-    mine = stack.at[y, :, pl.ds(pl.multiple_of(c * HALF, HALF), HALF)]
-    others = pl.ds(0, NZ - 1)
-    copies.spread([mine] * (NZ - 1), zbuf.at[z], zrecv, zs, zbuf.at[others])
-    copies.spread([cy.at[2]] * (NZ - 1), cz.at[z], crecv.at[0], zs, cz.at[others])
-    keep = pltpu.make_async_copy(mine, zbuf.at[z], local.at[0])
-    keep.start()
+    cz[z] = cy[2]
     keep.wait()
-    cz[z] = cy[2]
-    wait_recv(zbuf.at[others], zrecv)
+    wait_recv(zbuf.at[pl.ds(0, 2 * reach - 2)], zrecv.at[0])
+    wait_recv(zbuf.at[pl.ds(0, NZ - 1 - 2 * reach)], zrecv.at[3])
     for i in range(NZ):
         tmp[SHARD * i:SHARD * (i + 1), :] = zbuf[i].astype(F32)
     blk[...] = tmp[...].astype(BF)
@@ -170,24 +181,37 @@
     sibling = device(x, y, z, 1 - c)
     spot_own = pltpu.make_async_copy(blk, spot(0, 0), local.at[0])
     spot_own.start()
-    for d, j in ((1, 0), (-1, 1)):
+    for d, j in ((2, 2), (1, 0), (-1, 1)):
         copies.send(blk, spot(0, 0), frecv.at[j], first_to(d))
     for d, j in ((1, 0), (-1, 1)):
         copies.send(blk, spot(0, 0), srecv.at[0, j], second_to(d))
     copies.send(blk, spot(0, 0), sibrecv, sibling)
 
+    copies.spread([cy.at[2]] * (NZ - 1), cz.at[z], crecv.at[0], zs, cz.at[others])
+    for i, df in ((0, -1), (1, 1)):
+        wait_recv(spot(df, 0), frecv.at[i])
+        for d, j in ((1, 0), (-1, 1)):
+            copies.send(spot(df, 0), spot(df, 0), srecv.at[1 + i, j], second_to(d))
+        copies.send(spot(df, 0), spot(df, 0), sibrecv, sibling)
+
+    def relay(row, df):
+        for i, ds in ((0, -1), (1, 1)):
+            wait_recv(spot(df, ds), srecv.at[row, i])
+            copies.send(spot(df, ds, i), spot(df, ds, i), srecv.at[row, 2 + i], second_to(-ds))
+            copies.send(spot(df, ds), spot(df, ds), sibrecv, sibling)
+
+    wait_recv(spot(2, 0), frecv.at[2])
+    for d, j in ((2, 2), (1, 0), (-1, 1)):
+        copies.send(spot(2, 0), spot(2, 0), srecv.at[3, j], second_to(d))
+    copies.send(spot(2, 0), spot(2, 0), sibrecv, sibling)
+    relay(0, 0)
     wait_recv(cz.at[others], crecv.at[0])
     cy[0] = jnp.sum(cz[...], axis=0)
     for to in xs:
         copies.send(cy.at[0], cx.at[x], crecv.at[1], to)
 
-    for i, df in ((0, -1), (1, 1)):
-        wait_recv(spot(df, 0), frecv.at[i])
-        copies.send(spot(df, 0, i), spot(df, 0, i), frecv.at[2 + i], first_to(-df))
-        for d, j in ((1, 0), (-1, 1)):
-            copies.send(spot(df, 0), spot(df, 0), srecv.at[1 + i, j], second_to(d))
-        copies.send(spot(df, 0), spot(df, 0), sibrecv, sibling)
-
+    relay(1, -1)
+    relay(2, 1)
     wait_recv(cx.at[pl.ds(0, NX - 1)], crecv.at[1])
     got = cy[0]
     for d in range(1, NX):
@@ -197,29 +221,19 @@
     for to in dps:
         copies.send(cy.at[1], cd.at[me], crecv.at[2], to)
 
-    def relay(row, df):
-        for i, ds in ((0, -1), (1, 1)):
-            wait_recv(spot(df, ds), srecv.at[row, i])
-            copies.send(spot(df, ds, i), spot(df, ds, i), srecv.at[row, 2 + i], second_to(-ds))
-            copies.send(spot(df, ds), spot(df, ds), sibrecv, sibling)
-
-    relay(0, 0)
-    for i in (0, 1):
-        wait_recv(spot(2, 0, i), frecv.at[2 + i])
-    for d, j in ((1, 0), (-1, 1)):
-        copies.send(spot(2, 0), spot(2, 0), srecv.at[3, j], second_to(d))
-    copies.send(spot(2, 0), spot(2, 0), sibrecv, sibling)
-    relay(1, -1)
-    relay(2, 1)
-    relay(3, 2)
-    for row, df in ((0, 0), (1, -1), (2, 1), (3, 2)):
+    for i, ds in ((0, -1), (1, 1)):
+        wait_recv(spot(2, ds), srecv.at[3, i])
+        copies.send(spot(2, ds), spot(2, ds), sibrecv, sibling)
+    for row, df in ((0, 0), (1, -1), (2, 1)):
         for i in (0, 1):
             wait_recv(spot(df, 2, i), srecv.at[row, 2 + i])
         copies.send(spot(df, 2), spot(df, 2), sibrecv, sibling)
+    wait_recv(spot(2, 2), srecv.at[3, 2])
+    copies.send(spot(2, 2), spot(2, 2), sibrecv, sibling)
     spot_own.wait()
     wait_recv(full.at[:, :, pl.ds(pl.multiple_of((1 - c) * HALF, HALF), HALF)], sibrecv)
 
-    xr, xl, xo = mod(x + 1, NX), mod(x - 1, NX), mod(x + 2, NX)
+    rest = pl.ds(0, NX - 1)
     low = lane_low((COLS, 2 * PAIR))
     logit, slope = 0, 1
 
@@ -230,28 +244,25 @@
                 h = 2 * p + j
                 part[kind, h // HPX, h % HPX] = both[COLS * j:COLS * (j + 1)]
 
+    def over_x(kind):
+        copies.spread([part.at[kind, mod(x + d, NX)] for d in (2, 1, 3)], rx.at[kind, x], xrecv.at[kind], xs,
+                      rx.at[kind, rest])
+
     q[...] = (nn(normed[...], full[0]).astype(BF).astype(F32) * live[...]).astype(BF)
     k[...] = nn(normed[...], full[1]).astype(BF)
     partial(q, k, logit)
-    copies.send(part.at[logit, xo], ra, xrecv.at[0], right)
-    copies.send(part.at[logit, xl], rd, xrecv.at[3], left)
+    over_x(logit)
     v[...] = nn(normed[...], full[2]).astype(BF)
     ga[...] = nt(gm[...], full[3]).astype(BF)
     partial(ga, v, slope)
-    copies.send(part.at[slope, xo], rb, xrecv.at[1], left)
-    copies.send(part.at[slope, xr], rc, xrecv.at[2], right)
-    wait_recv(ra, xrecv.at[0])
-    ta[...] = (part[logit, xr].astype(F32) + ra[...].astype(F32)).astype(BF)
-    copies.send(ta, re, xrecv.at[4], right)
-    wait_recv(rb, xrecv.at[1])
-    tb[...] = (part[slope, xl].astype(F32) + rb[...].astype(F32)).astype(BF)
-    copies.send(tb, rf, xrecv.at[5], left)
-
-    for kind, one, sem_one, two, sem_two in ((logit, rd, 3, re, 4), (slope, rc, 2, rf, 5)):
-        wait_recv(one, xrecv.at[sem_one])
-        wait_recv(two, xrecv.at[sem_two])
+    over_x(slope)
+
+    for kind in (logit, slope):
+        wait_recv(rx.at[kind, rest], xrecv.at[kind])
         for h in range(HPX):
-            value = part[kind, x, h].astype(F32) + one[h].astype(F32) + two[h].astype(F32)
+            value = part[kind, x, h].astype(F32)
+            for d in range(1, NX):
+                value = value + rx[kind, mod(x + d, NX), h].astype(F32)
             tf[kind, :, IPZ * h:IPZ * (h + 1), :] = value.reshape(NZ, IPZ, COLS)
         tz[kind] = tf[kind].astype(BF)
         copies.spread([tz.at[kind, mod(z + d, NZ)] for d in far], rz.at[kind, z], rrecv.at[kind], zs,
@@ -282,18 +293,7 @@
         got = oz[kind].astype(F32)
         for h in range(HPX):
             soft[kind, x, h] = got[:, IPZ * h:IPZ * (h + 1), :].reshape(COLS, COLS).astype(BF)
-        ahead, behind = (right, left) if kind == logit else (left, right)
-        copies.send(soft.at[kind, x], soft.at[kind, x], arecv.at[kind, 0], ahead)
-        copies.send(soft.at[kind, x], soft.at[kind, x], arecv.at[kind, 1], behind)
-
-    def collect(kind):
-        near = xl if kind == logit else xr
-        wait_recv(soft.at[kind, near], arecv.at[kind, 0])
-        copies.send(soft.at[kind, near], soft.at[kind, near], arecv.at[kind, 2], right if kind == logit else left)
-
-    def finish(kind):
-        wait_recv(soft.at[kind, xr if kind == logit else xl], arecv.at[kind, 1])
-        wait_recv(soft.at[kind, xo], arecv.at[kind, 2])
+        copies.spread([soft.at[kind, x]] * (NX - 1), soft.at[kind, x], arecv.at[kind], xs, soft.at[kind, rest])
 
     def apply(kind, across, across_to, down, down_to):
         for p in range(HEADS // 2):
@@ -306,13 +306,11 @@
                 dst[0:COLS, PAIR * p:PAIR * (p + 1)] = value[:, 0:PAIR]
                 dst[COLS:2 * COLS, PAIR * p:PAIR * (p + 1)] = value[:, PAIR:2 * PAIR]
 
-    collect(logit)
-    collect(slope)
-    finish(logit)
+    wait_recv(soft.at[logit, rest], arecv.at[logit])
     apply(logit, v, att, ga, gv)
     mixed[...] = (hidden[...].astype(F32) + live[...] * nn(att[...], full[3])).astype(BF)
     acc = nt(gv[...], full[2])
-    finish(slope)
+    wait_recv(soft.at[slope, rest], arecv.at[slope])
     apply(slope, k, gq, q, gk)
     acc = acc + nt(gq[...], full[0]) * live[...] + nt(gk[...], full[1])
     scaled = acc * gain[...].reshape(1, D)
@@ -334,7 +332,6 @@
     dma = pltpu.SemaphoreType.DMA
     tokens = jax.ShapeDtypeStruct((2 * COLS, D), BF)
     act, col = pltpu.VMEM((2 * COLS, D), BF), pltpu.VMEM((2 * COLS, 1), F32)
-    quarter = pltpu.VMEM((HPX, COLS, COLS), BF)
     chunks = pltpu.VMEM((2, NZ, CHUNK, COLS), BF)
     heads = pltpu.VMEM((2, NX, HPX, COLS, COLS), BF)
     return pl.pallas_call(
@@ -355,10 +352,10 @@
             pltpu.VMEM((SLAB, HALF), BF),
             pltpu.VMEM((2 * COLS, D), F32), col, act, act, col, col,
             act, act, act, act, act, act, act, act,
-            heads, quarter, quarter, quarter, quarter, quarter, quarter, quarter, quarter,
+            heads, heads,
             pltpu.VMEM((2, NZ, CHUNK, COLS), F32), chunks, chunks, pltpu.VMEM((2, CHUNK, COLS), BF), chunks, heads,
-            dma((4,)), dma, dma((3,)), dma((4,)), dma((4, 4)), dma, dma((6,)), dma((2,)), dma((2,)), dma((2, 3)),
-            dma((80,)), dma((6,)),
+            dma((4,)), dma((4,)), dma((3,)), dma((3,)), dma((4, 4)), dma, dma((2,)), dma((2,)), dma((2,)), dma((2,)),
+            dma((80,)), dma((12,)),
         ],
         compiler_params=pltpu.CompilerParams(collective_id=0, has_side_effects=True),
     )(depths, hidden, masked, gain, wq, wk, wv, wo, cot)

time: 94.2 us -> 88 us (0.934); the launches traced: 92.7 us -> 87.7 us
  Pallas kernels: 88.9 us -> 83.9 us
    pallas_call x1, Pallas kernels: 88.9 us -> 83.9 us  [step(): pl.pallas_call(step_kernel, name='step', out_shape=(tokens, tokens), in_s...]
where the time goes in v3:
time: 88 us; the launch traced here: 87.7 us
  Pallas kernels  83.9 us (95%)
  local copies, waits for them, and re-layouts  2.57 us (3%)
  between operations  1.3 us (1%)
    pallas_call x1, Pallas kernels, step(): pl.pallas_call(step_kernel, name='step', out_shape=(tokens, tokens), in_s...  83.9 us
    unnamed x4, local copies, waits for them, and re-layouts  2.57 us

profile of v3, /device:TPU:1, one launch (start us, length us, event | category | flops | bytes accessed | tf_op | source)
XLA Modules:
  0.0 87.7 jit_solution(4293160313976259703)
XLA Ops:
  1.3 83.9 %step.1 = (bf16[256,768]{1,0:T(8,128)(2,1)}, bf16[256,768]{1,0:T(8,128)(2,1)}) custom-call(s32[1]{0:T(128)S(6)} %copy.13.depth, bf16[256,768]{1,0:T(8,128)(2,1)} %bitcast.7, s32[2,128]{1,0:T(2,128)} %bitcast.9, f32[768]{0:T(1024)} %gain.1, bf16[12,768]{1,0:T(8,128)(2,1)} %wq.1, bf16[12,768]{1,0:T(8,128)(2,1)} %wk.1, bf16[12,768]{1,0:T(8,128)(2,1)} %wv.1, ...), custom_call_target="tpu_custom_call" | custom-call | tf_op jit(solution)/shard_map/step/pallas_call | solution.py:337
  85.2 0.0 copy-start
  85.2 1.8 %copy.14 = bf16[1,2,128,768]{3,2,1,0:T(8,128)(2,1)} copy(bf16[1,2,128,768]{3,2,1,0:T(8,128)(2,1)} %bitcast.6) | data formatting | bytes 786432
  87.0 0.0 copy-done
  87.0 0.7 copy.15
Async XLA Ops:
  85.2 1.8 %copy-start = (bf16[256,768]{1,0:T(8,128)(2,1)S(1)}, bf16[256,768]{1,0:T(8,128)(2,1)}, u32[]{:S(2)}) copy-start(bf16[256,768]{1,0:T(8,128)(2,1)} %get-tuple-element.5) | copy-start | bytes 1179652
